TPU v7x, 32 devices: a whole 2x2x4 slice. The times are simulated.
32 devices in a mesh: row: 4 (over z), col: 8 (over y, x, core).
Axes of the slice: x: 2, y: 2, z: 4, core: 2. Of those that a mesh axis runs over, the one named last changes fastest.
Arguments:
- features: bfloat16 [12, 4, 256, 256], P(None, 'row', 'col'), may hold values from -6 to 6
Outputs:
- schur: float32 [12, 4, 256, 6, 8, 256], P(None, 'row', None, None, 'col')
- panels: float32 [12, 4, 256, 512], P(None, 'row')
All inputs are finite; a program needn't handle non-finite values.
Results may differ from a plain program's by a relative error of at most 0.0033.
Values may be sent and summed in bfloat16 or wider, within the bound.
A program may use at most 128 MiB of HBM per device.

v0:
```python
import jax
import jax.numpy as jnp
from jax import lax
from jax.sharding import PartitionSpec as P

kernel_gain = 2.0
epsilon = 1e-06


def spread(value, axis, source):
    kept = jnp.where(lax.axis_index(axis) == source, value, 0).astype(value.dtype)
    return lax.psum(kept, axis)


def front_kernel(points, tile_ids, front_points, tile_len):
    products = lax.dot_general(
        points, front_points, (((1,), (1,)), ((), ())), preferred_element_type=jnp.float32
    )
    values = jnp.exp(kernel_gain * (products - 1.0))
    coincide = (tile_ids[:, None] == jnp.arange(2, dtype=jnp.int32)[None, :]).astype(jnp.float32)
    identity = jnp.eye(tile_len, dtype=jnp.float32)
    nugget = (coincide[:, None, :, None] * identity[None, :, None, :]).reshape(values.shape)
    return values + nugget


def mark_tiles(solved, tile_ids, factor, panel_index, tile_len):
    pieces = solved.reshape(tile_ids.shape[0], tile_len, tile_len)
    marker = tile_ids[:, None, None]
    pieces = jnp.where(
        marker == panel_index,
        factor[None],
        jnp.where(marker < panel_index, jnp.zeros_like(pieces), pieces),
    )
    return pieces.reshape(tile_ids.shape[0] * tile_len, tile_len)


def both_factors(
    points, tile_ids, front_points, first_factor, second_factor, first_front, tile_len
):
    block = front_kernel(points, tile_ids, front_points, tile_len)
    solved = lax.linalg.triangular_solve(
        first_factor, block[:, :tile_len], left_side=False, lower=True, transpose_a=True
    )
    first_part = mark_tiles(solved, tile_ids, first_factor, 0, tile_len)
    reduced = block[:, tile_len:] - jnp.dot(
        first_part, first_front[tile_len:].T, precision=lax.Precision.HIGHEST
    )
    solved_next = lax.linalg.triangular_solve(
        second_factor, reduced, left_side=False, lower=True, transpose_a=True
    )
    second_part = mark_tiles(solved_next, tile_ids, second_factor, 1, tile_len)
    return jnp.concatenate([first_part, second_part], axis=1)


def per_device(features):
    row_count = lax.axis_size("row")
    col_count = lax.axis_size("col")
    own_row = lax.axis_index("row")
    own_col = lax.axis_index("col")
    floated = features.astype(jnp.float32)
    unit_rows = (
        floated * lax.rsqrt(jnp.sum(floated * floated, axis=-1, keepdims=True) + epsilon)
    ).astype(jnp.bfloat16)
    gathered = lax.all_gather(unit_rows, "col", axis=2, tiled=True)
    local_tiles = gathered.shape[0]
    tile_len = gathered.shape[2]
    feat_width = gathered.shape[3]
    stride = col_count // row_count
    grouped = gathered.reshape(local_tiles // stride, stride, tile_len, feat_width)
    chosen = lax.dynamic_index_in_dim(grouped, own_col // row_count, 1, keepdims=False)
    column_feats = spread(chosen, "row", own_col % row_count)
    across_tiles = column_feats.shape[0]
    row_points = gathered.reshape(local_tiles * tile_len, feat_width)
    col_points = column_feats.reshape(across_tiles * tile_len, feat_width)
    products = lax.dot_general(
        row_points, col_points, (((1,), (1,)), ((), ())), preferred_element_type=jnp.float32
    )
    row_global = jnp.arange(local_tiles, dtype=jnp.int32) * row_count + own_row
    col_global = jnp.arange(across_tiles, dtype=jnp.int32) * col_count + own_col
    coincide = (row_global[:, None] == col_global[None, :]).astype(jnp.float32)
    identity = jnp.eye(tile_len, dtype=jnp.float32)
    nugget = coincide[:, None, :, None] * identity[None, :, None, :]
    kernel = (
        jnp.exp(kernel_gain * (products - 1.0)).reshape(
            local_tiles, tile_len, across_tiles, tile_len
        )
        + nugget
    ).reshape(local_tiles * tile_len, across_tiles * tile_len)
    leading = lax.all_gather(gathered[0:1], "row", axis=1, tiled=True)
    front_points = leading[0, 0:2].reshape(2 * tile_len, feat_width)
    front_ids = jnp.arange(2, dtype=jnp.int32)
    front_block = front_kernel(front_points, front_ids, front_points, tile_len)
    first_factor = jnp.linalg.cholesky(front_block[:tile_len, :tile_len])
    first_solved = lax.linalg.triangular_solve(
        first_factor, front_block[:, :tile_len], left_side=False, lower=True, transpose_a=True
    )
    first_front = mark_tiles(first_solved, front_ids, first_factor, 0, tile_len)
    front_next = front_block[:, tile_len:] - jnp.dot(
        first_front, first_front[tile_len:].T, precision=lax.Precision.HIGHEST
    )
    second_factor = jnp.linalg.cholesky(front_next[tile_len:])
    both_rows = both_factors(
        row_points, row_global, front_points, first_factor, second_factor, first_front, tile_len
    )
    both_cols = both_factors(
        col_points, col_global, front_points, first_factor, second_factor, first_front, tile_len
    )
    schur = kernel - lax.dot_general(
        both_rows,
        both_cols,
        (((1,), (1,)), ((), ())),
        precision=lax.Precision.HIGHEST,
        preferred_element_type=jnp.float32,
    )
    return (
        schur.reshape(local_tiles, 1, tile_len, across_tiles, 1, tile_len),
        both_rows.reshape(local_tiles, 1, tile_len, 2 * tile_len),
    )


def solution(mesh):
    return jax.shard_map(
        per_device,
        mesh=mesh,
        in_specs=(P(None, "row", "col", None),),
        out_specs=(P(None, "row", None, None, "col", None), P(None, "row", None, None)),
        check_vma=False,
    )
```

profile of v0, /device:TPU:0, one launch (start us, length us, event | category | flops | bytes accessed | tf_op | source)
XLA Modules:
  0.0 410.6 jit_solution(9091056674707095724)
XLA Ops:
  23.2 10.8 %broadcast_multiply_fusion = f32[12,256,6,256]{3,2,1,0:T(8,128)} fusion(f32[256,256]{1,0:T(8,128)S(1)} %fusion.34, f32[12,6]{1,0:T(8,128)S(1)} %compare_convert_fusion), kind=kLoop, calls=%fused_computation.5 | loop fusion | flops 4718592 | bytes 19136800 | tf_op jit(solution)/shard_map/mul | solution.py:82
  34.0 20.6 %copy.48 = f32[384,8,6,256]{3,1,2,0:T(8,128)} copy(f32[384,8,6,256]{3,2,1,0:T(8,128)} %bitcast.142) | data formatting | bytes 37748736
  55.5 28.3 %all_gather.7 = bf16[1,4,256,256]{3,2,0,1:T(8,128)(2,1)S(1)} all-gather(bf16[1,1,256,256]{3,2,0,1:T(8,128)(2,1)S(1)} %slice.183), channel_id=1, replica_groups=mesh['row'=4,'col'=8] {'row'}, dimensions={1}, use_global_device_ids=true | all-gather | bytes 655360 | tf_op jit(solution)/shard_map/all_gather | solution.py:89
  85.2 11.7 %cholesky.130 = f32[128,128]{1,0:T(8,128)S(1)} custom-call(f32[128,128]{1,0:T(8,128)S(1)} %cholesky.194), custom_call_target="Cholesky" | custom-call | tf_op jit(solution)/shard_map/jit(cholesky)/cholesky | solution.py:93
  96.9 9.8 %custom-call.21 = f32[1,128,128]{1,2,0:T(8,128)S(1)} custom-call(f32[1,128,128]{2,1,0:T(8,128)S(1)} %get-tuple-element.82), custom_call_target="InvertDiagBlocksLowerTriangular" | custom-call | tf_op jit(solution)/shard_map/jit(cholesky)/cholesky | solution.py:93
  107.3 11.7 %cholesky.147 = f32[128,128]{1,0:T(8,128)S(1)} custom-call(f32[128,128]{1,0:T(8,128)S(1)} %convolution_subtract_fusion.8), custom_call_target="Cholesky" | custom-call | tf_op jit(solution)/shard_map/jit(cholesky)/cholesky | solution.py:93
  121.1 4.0 while.9
  125.6 19.7 %custom-call.22 = f32[2,128,128]{1,2,0:T(8,128)S(1)} custom-call(f32[2,128,128]{2,1,0:T(8,128)S(1)} %get-tuple-element.41), custom_call_target="InvertDiagBlocksLowerTriangular" | custom-call | tf_op jit(solution)/shard_map/triangular_solve/custom-call.0 | solution.py:41
  150.8 4.7 %exponential_add_fusion = f32[3072,512]{1,0:T(8,128)S(1)} fusion(f32[3072,512]{1,0:T(8,128)} %bitcast.144, bf16[3072,256]{1,0:T(8,128)(2,1)} %bitcast.154, bf16[512,256]{1,0:T(8,128)(2,1)} %bitcast.160), kind=kOutput, calls=%fused_computation.11 | convolution fusion | flops 810024960 | bytes 14417920 | tf_op jit(solution)/shard_map/dot_general | solution.py:16
  157.1 3.7 convolution_subtract_fusion.2
  166.4 8.7 %convolution_subtract_fusion = f32[3072,256]{1,0:T(8,128)} fusion(f32[3072,256]{0,1:T(8,128)S(1)} %fusion.7, f32[3072,512]{1,0:T(8,128)} %copy-done.1, f32[2,256,256]{2,1,0:T(8,128)} %bitcast.167, f32[256,256]{1,0:T(8,128)S(1)} %get-tuple-element.70, pred[1]{0:T(512)(128)(4,1)} %slice.192), kind=kOutput, calls=%fused_computation.12 | convolution fusion | flops 2416771072 | bytes 9961984 | tf_op jit(solution)/shard_map/dot_general | solution.py:45
  181.3 13.2 %cholesky.164 = f32[128,128]{1,0:T(8,128)} custom-call(f32[128,128]{1,0:T(8,128)} %cholesky.197), custom_call_target="Cholesky" | custom-call | tf_op jit(solution)/shard_map/jit(cholesky)/cholesky | solution.py:101
  196.6 11.3 %custom-call.23 = f32[1,128,128]{1,2,0:T(8,128)} custom-call(f32[1,128,128]{2,1,0:T(8,128)} %get-tuple-element.78), custom_call_target="InvertDiagBlocksLowerTriangular" | custom-call | tf_op jit(solution)/shard_map/jit(cholesky)/cholesky | solution.py:101
  212.9 13.2 %cholesky.181 = f32[128,128]{1,0:T(8,128)} custom-call(f32[128,128]{1,0:T(8,128)} %convolution_subtract_fusion.7), custom_call_target="Cholesky" | custom-call | tf_op jit(solution)/shard_map/jit(cholesky)/cholesky | solution.py:101
  232.0 6.9 %while.10 = (s32[]{:T(128)}, f32[256,256]{1,0:T(8,128)}, s32[2,2]{1,0:T(2,128)S(1)}, f32[2,128,128]{2,1,0:T(8,128)}, s32[]{:T(128)}) while((s32[]{:T(128)}, f32[256,256]{1,0:T(8,128)}, s32[2,2]{1,0:T(2,128)S(1)}, f32[2,128,128]{2,1,0:T(8,128)}, s32[]{:T(128)}) %tuple.77), condition=%wide.while_cond.clone, body=%wide.while_body.clone.sunk | while | flops 2 | bytes 132205 | solution.py:48
  238.8 21.3 %custom-call.24 = f32[2,128,128]{1,2,0:T(8,128)} custom-call(f32[2,128,128]{2,1,0:T(8,128)} %get-tuple-element.42), custom_call_target="InvertDiagBlocksLowerTriangular" | custom-call | tf_op jit(solution)/shard_map/triangular_solve/custom-call.0 | solution.py:48
  274.9 3.6 copy.38
  281.6 3.7 convolution_subtract_fusion.1
  288.9 4.0 copy.42
  292.9 6.4 %maximum_bitcast_fusion = f32[12,1,256,512]{3,2,1,0:T(8,128)} fusion(f32[12,1,256,256]{3,2,0,1:T(8,128)} %bitcast.153, f32[12,1,256,256]{3,2,0,1:T(8,128)} %bitcast.152), kind=kLoop, calls=%fused_computation.10 | loop fusion | flops 1572864 | bytes 12582912
  299.3 8.7 %all-reduce.3.cloned.1.call-done = bf16[1536,256]{1,0:T(8,128)(2,1)} async-done(((bf16[1536,256]{1,0:T(8,128)(2,1)}), bf16[1536,256]{1,0:T(8,128)(2,1)}) %all-reduce.3.cloned.1.call-update) | async-done | bytes 786448 | tf_op jit(solution)/shard_map/psum | solution.py:12
  323.8 33.5 %fusion = f32[3072,1536]{1,0:T(8,128)} fusion(f32[3072,256]{0,1:T(8,128)S(1)} %copy-done, f32[3072,256]{0,1:T(8,128)S(1)} %fusion.7, f32[1536,256]{0,1:T(8,128)S(1)} %fusion.17, f32[1536,256]{0,1:T(8,128)S(1)} %fusion.16), kind=kOutput, calls=%fused_computation.6 | convolution fusion | flops 28993388544 | bytes 28311552 | tf_op jit(solution)/shard_map/dot_general | solution.py:108
  357.3 18.5 %add_subtract_fusion = f32[3072,1536]{1,0:T(8,128)} fusion(f32[3072,1536]{1,0:T(8,128)} %fusion, f32[3072,1536]{1,0:T(8,128)} %bitcast.143, bf16[3072,256]{1,0:T(8,128)(2,1)} %bitcast.156, bf16[1536,256]{1,0:T(8,128)(2,1)} %all-reduce.3.cloned.1.call-done), kind=kOutput, calls=%fused_computation.4 | convolution fusion | flops 2434793472 | bytes 58982400 | tf_op jit(solution)/shard_map/dot_general | solution.py:75
  375.7 27.8 %reshape.395 = f32[12,1,256,6,1,256]{5,4,3,2,1,0:T(1,128)} reshape(f32[3072,1536]{1,0:T(8,128)} %add_subtract_fusion) | data formatting | bytes 37748736 | tf_op jit(solution)/shard_map/reshape | solution.py:116
  (169 shorter events, 98.2 us)
Async XLA Ops:
  7.2 47.4 %all-gather.2.cloned.1.call-start = ((), (), s32[]{:S(2)}) async-start(), calls=%async_computation | async-start | bytes 1769472 | tf_op jit(solution)/shard_map/all_gather | solution.py:64
  10.0 298.0 %all-reduce.3.cloned.1.call-start = ((), (), s32[]{:S(2)}) async-start(), calls=%async_computation.1 | async-start | bytes 1572864 | tf_op jit(solution)/shard_map/psum | solution.py:12
  84.9 60.9 %copy-start.6 = (f32[512,512]{0,1:T(8,128)}, f32[512,512]{0,1:T(8,128)S(1)}, u32[]{:S(2)}) copy-start(f32[512,512]{0,1:T(8,128)S(1)} %fusion.20) | copy-start | bytes 3145732
  125.1 22.7 %copy-start.12 = (f32[256,256]{1,0:T(8,128)}, f32[256,256]{1,0:T(8,128)S(1)}, u32[]{:S(2)}) copy-start(f32[256,256]{1,0:T(8,128)S(1)} %get-tuple-element.191) | copy-start | bytes 786436
  145.9 1.9 copy-start.9
  146.9 0.9 copy-start.13
  155.5 5.3 %copy-start.1 = (f32[3072,512]{1,0:T(8,128)}, f32[3072,512]{1,0:T(8,128)S(1)}, u32[]{:S(2)}) copy-start(f32[3072,512]{1,0:T(8,128)S(1)} %exponential_add_fusion) | copy-start | bytes 18874372
  157.1 5.3 %copy-start.3 = (f32[3072,256]{0,1:T(8,128)S(1)}, f32[3072,256]{0,1:T(8,128)}, u32[]{:S(2)}) copy-start(f32[3072,256]{0,1:T(8,128)} %copy.34) | copy-start | bytes 9437188
  162.9 2.4 copy-start.22
  166.4 8.8 %copy-start.10 = (f32[512,256]{1,0:T(8,128)S(1)}, f32[512,256]{1,0:T(8,128)}, u32[]{:S(2)}) copy-start(f32[512,256]{1,0:T(8,128)} %pad_maximum_fusion) | copy-start | bytes 1572868
  166.4 10.0 %slice-start = ((f32[512,512]{0,1:T(8,128)}), f32[512,256]{0,1:T(8,128)S(1)}, s32[]{:S(2)}) async-start(f32[512,512]{0,1:T(8,128)} %copy-done.6), calls=%async_computation.2 | async-start | bytes 1048576 | tf_op jit(solution)/shard_map/slice | solution.py:98
  175.1 56.8 %copy-start.24 = (s32[2,2]{1,0:T(2,128)S(1)}, s32[2,2]{1,0:T(2,128)}, u32[]{:S(2)}) copy-start(s32[2,2]{1,0:T(2,128)} %copy-done.23) | copy-start | bytes 52
  278.4 3.1 copy-start.2
  281.5 3.7 copy-start.15
  281.5 5.3 %copy-start.4 = (f32[3072,256]{0,1:T(8,128)S(1)}, f32[3072,256]{0,1:T(8,128)}, u32[]{:S(2)}) copy-start(f32[3072,256]{0,1:T(8,128)} %copy.38) | copy-start | bytes 9437188
  311.0 4.1 copy-start.8
  311.0 4.1 copy-start.19
  311.0 4.1 copy-start.20
  314.1 1.2 copy-start.11
  315.3 3.4 copy-start.16
  318.7 4.1 copy-start.7
  318.7 4.1 copy-start.17
  318.7 4.1 copy-start.18
  321.9 1.9 copy-start
  (4 other events, 2.6 us)
Sparse Core Ops, SparseCore 0:
  10.4 28.3 all-gather.1
  262.3 45.6 all-reduce.2
where the time goes:
time: 419 us; the launch traced here: 411 us
  other arithmetic  151 us (36%)
  local copies, waits for them, and re-layouts  103 us (25%)
  matrix products  102 us (24%)
  blocking collectives  28.3 us (7%)
  between operations  17.6 us (4%)
  waiting for transfers between devices  8.71 us (2%)
    another operation x7, other arithmetic, per_device(): second_factor = jnp.linalg.cholesky(front_next[tile_len:])  41.9 us
    another operation x6, other arithmetic, per_device(): first_factor = jnp.linalg.cholesky(front_block[:tile_len, :tile_len])  34 us
    dot_general x1, matrix products, per_device(): lax.dot_general(both_rows, both_cols, (((1,), (1,)), ((), ())), precision...  33.5 us
    unnamed x54, local copies, waits for them, and re-layouts  28.9 us
    all_gather x1, blocking collectives, per_device(): leading = lax.all_gather(gathered[0:1], 'row', axis=1, tiled=True)  28.3 us
    reshape x1, local copies, waits for them, and re-layouts, per_device(): schur.reshape(local_tiles, 1, tile_len, across_tiles, 1, tile_len)  27.8 us
    another operation x2, other arithmetic, both_factors(): lax.linalg.triangular_solve(second_factor, reduced, left_side=False, lowe...  23.1 us
    broadcast_in_dim x16, local copies, waits for them, and re-layouts, mark_tiles(): jnp.where(marker == panel_index, factor[None], jnp.where(marker < panel_i...  20.7 us
  transfers between devices with their start and end apart: 2, of which 1 were waited for; matrix products, arithmetic and copies ran while one was open for 20% of the time, Pallas kernels for 0%

commit v1 on v0

v1 whole, which is shorter than its diff:
```python
import functools
import math

import jax
import jax.numpy as jnp
from jax import lax
from jax.experimental import pallas as pl
from jax.experimental.pallas import tpu as pltpu
from jax.sharding import PartitionSpec as P

kernel_gain = 2.0
epsilon = 1e-06
LEAF = 128
SUB = 8
gain2 = kernel_gain / math.log(2.0)
BF = jnp.bfloat16
F32 = jnp.float32
NT = (((1,), (1,)), ((), ()))
NN = (((1,), (0,)), ((), ()))
TN = (((0,), (0,)), ((), ()))


def split(x):
    hi = x.astype(BF)
    return hi, (x - hi.astype(F32)).astype(BF)


def dot(a, b, dims):
    return lax.dot_general(a, b, dims, preferred_element_type=F32)


def dot3(a, b, dims):
    ah, al = a
    bh, bl = b
    return dot(ah, bh, dims) + (dot(ah, bl, dims) + dot(al, bh, dims))


def gram(a, b):
    return jnp.exp2(gain2 * dot(a, b, NT) - gain2)


def eye(n):
    return (
        lax.broadcasted_iota(jnp.int32, (n, n), 0) == lax.broadcasted_iota(jnp.int32, (n, n), 1)
    ).astype(F32)


def leaf(block):
    groups = LEAF // SUB
    ident = eye(LEAF)
    a = [block[g * SUB:(g + 1) * SUB] for g in range(groups)]
    m = [ident[g * SUB:(g + 1) * SUB] for g in range(groups)]
    sub = lax.broadcasted_iota(jnp.int32, (SUB, LEAF), 0)

    def lane(x, at):
        return jnp.broadcast_to(x[:, at:at + 1], (SUB, LEAF))

    def row(x, at):
        return jnp.broadcast_to(x[at:at + 1, :], (SUB, LEAF))

    for p in range(groups):
        ra, rm = a[p], m[p]
        c = [lane(ra, p * SUB + k) for k in range(SUB)]
        scale, ua, um, uc = [], [], [], []
        for j in range(SUB):
            r = lax.rsqrt(row(c[j], j))
            below = jnp.where(sub > j, c[j] * r, 0.0)
            wa, wm = row(ra, j) * r, row(rm, j) * r
            wc = [row(c[k], j) * r for k in range(j + 1, SUB)]
            scale.append(r)
            ua.append(wa)
            um.append(wm)
            uc.append(wc)
            for k in range(j + 1, SUB):
                c[k] = c[k] - below * wc[k - j - 1]
            ra = jnp.where(sub == j, wa, ra - below * wa)
            rm = jnp.where(sub == j, wm, rm - below * wm)
        a[p], m[p] = ra, rm
        for g in range(p + 1, groups):
            c = [lane(a[g], p * SUB + k) for k in range(SUB)]
            for j in range(SUB):
                l = c[j] * scale[j]
                for k in range(j + 1, SUB):
                    c[k] = c[k] - l * uc[j][k - j - 1]
                a[g] = a[g] - l * ua[j]
                m[g] = m[g] - l * um[j]
    return jnp.concatenate(m, axis=0)


def factor_body(front_ref, hi_ref, lo_ref, work):
    n = front_ref.shape[0]
    blocks = n // LEAF
    f = front_ref[...]
    work[:, 0:n] = gram(f, f) + eye(n)
    work[:, n:2 * n] = eye(n)

    def step(b, carry):
        here = pl.ds(pl.multiple_of(b * LEAF, LEAF), LEAF)
        inverse = leaf(work[here, here])
        for at in range(blocks):
            lo_at, up = at * LEAF, (at + 1) * LEAF

            @pl.when(b == at)
            def _():
                inv = split(inverse)
                if at:
                    work[lo_at:up, n:n + lo_at] = dot3(
                        inv, split(work[lo_at:up, n:n + lo_at]), NN
                    )
                work[lo_at:up, n + lo_at:n + up] = inverse
                if up < n:
                    right = dot3(inv, split(work[lo_at:up, up:n]), NN)
                    rs = split(right)
                    work[up:n, up:n] = work[up:n, up:n] - dot3(rs, rs, TN)
                    ms = split(work[lo_at:up, n:n + up])
                    work[up:n, n:n + up] = work[up:n, n:n + up] - dot3(rs, ms, TN)

        return carry

    lax.fori_loop(0, blocks, step, 0)
    hi, lo = split(work[:, n:2 * n])
    hi_ref[...] = hi
    lo_ref[...] = lo


def factor(front):
    n = front.shape[0]
    shape = jax.ShapeDtypeStruct((n, n), BF)
    return pl.pallas_call(
        factor_body,
        out_shape=(shape, shape),
        in_specs=[pl.BlockSpec(memory_space=pltpu.VMEM)],
        out_specs=(pl.BlockSpec(memory_space=pltpu.VMEM),) * 2,
        scratch_shapes=[pltpu.VMEM((n, 2 * n), F32)],
        cost_estimate=pl.CostEstimate(flops=int(2e10), bytes_accessed=int(5e7), transcendentals=0),
        name="factor",
    )(front)


def panel_of(points, tile_id, front, hi_ref, lo_ref, tile_len):
    n = front.shape[0]
    values = gram(points, front)
    at = lax.broadcasted_iota(jnp.int32, values.shape, 0) + tile_id * tile_len
    values = values + (at == lax.broadcasted_iota(jnp.int32, values.shape, 1)).astype(F32)
    hi, lo = split(values)
    t = tile_len
    first = dot3((hi[:, :t], lo[:, :t]), (hi_ref[:t, :t], lo_ref[:t, :t]), NT)
    second = dot3((hi, lo), (hi_ref[t:, :], lo_ref[t:, :]), NT)
    return jnp.concatenate([first, second], axis=1)


def schur_body(ids, rows_ref, cols_ref, front_ref, hi_ref, lo_ref, out_ref, panel_ref, q_ref):
    tile_len = rows_ref.shape[0]
    across = cols_ref.shape[0] // tile_len
    own_row, row_count, own_col, col_count = ids[0], ids[1], ids[2], ids[3]
    a = pl.program_id(0)
    chunks = across * tile_len // LEAF

    @pl.when(a == 0)
    def _():
        def one(b, carry):
            here = pl.ds(pl.multiple_of(b * tile_len, tile_len), tile_len)
            hi, lo = split(
                panel_of(
                    cols_ref[here, :], b * col_count + own_col, front_ref[...], hi_ref, lo_ref,
                    tile_len,
                )
            )
            q_ref[here, :] = jnp.concatenate([hi, lo[:, :LEAF], hi[:, :LEAF]], axis=1)
            return carry

        lax.fori_loop(0, across, one, 0)

    tile_id = a * row_count + own_row
    points = rows_ref[...]
    panel = panel_of(points, tile_id, front_ref[...], hi_ref, lo_ref, tile_len)
    panel_ref[...] = panel
    hi, lo = split(panel)
    p = jnp.concatenate([hi, hi[:, :LEAF], lo[:, :LEAF]], axis=1)
    per = tile_len // LEAF
    for b in range(across):
        here = slice(b * tile_len, (b + 1) * tile_len)
        s = gram(points, cols_ref[here, :]) - dot(p, q_ref[here, :], NT)
        for k in range(per):
            out_ref[pl.ds(b * per + k, tile_len, stride=chunks), :] = s[:, k * LEAF:(k + 1) * LEAF]

        @pl.when(tile_id == b * col_count + own_col)
        def _():
            ident = eye(tile_len)
            for k in range(per):
                at = pl.ds(b * per + k, tile_len, stride=chunks)
                out_ref[at, :] = out_ref[at, :] + ident[:, k * LEAF:(k + 1) * LEAF]


def schur(ids, row_points, col_points, front, hi, lo, tile_len):
    rows, feat = row_points.shape
    cols = col_points.shape[0]
    n = front.shape[0]
    chunks = cols // LEAF

    def whole(shape):
        return pl.BlockSpec(shape, lambda a, ids: (0, 0))

    return pl.pallas_call(
        schur_body,
        out_shape=(
            jax.ShapeDtypeStruct((rows * chunks, LEAF), F32),
            jax.ShapeDtypeStruct((rows, n), F32),
        ),
        grid_spec=pltpu.PrefetchScalarGridSpec(
            num_scalar_prefetch=1,
            grid=(rows // tile_len,),
            in_specs=[
                pl.BlockSpec((tile_len, feat), lambda a, ids: (a, 0)),
                whole((cols, feat)),
                whole((n, feat)),
                whole((n, n)),
                whole((n, n)),
            ],
            out_specs=(
                pl.BlockSpec((tile_len * chunks, LEAF), lambda a, ids: (a, 0)),
                pl.BlockSpec((tile_len, n), lambda a, ids: (a, 0)),
            ),
            scratch_shapes=[pltpu.VMEM((cols, n + 2 * LEAF), BF)],
        ),
        compiler_params=pltpu.CompilerParams(dimension_semantics=("arbitrary",)),
        name="schur",
    )(ids, row_points, col_points, front, hi, lo)


def per_device(features):
    row_count = lax.axis_size("row")
    col_count = lax.axis_size("col")
    own_row = lax.axis_index("row")
    own_col = lax.axis_index("col")
    floated = features.astype(F32)
    unit = (
        floated * lax.rsqrt(jnp.sum(floated * floated, axis=-1, keepdims=True) + epsilon)
    ).astype(BF)
    leading = lax.all_gather(unit[0, 0], ("row", "col"))
    piece, feat = leading.shape[1:]
    local_tiles = unit.shape[0]
    tile_len = piece * col_count
    front = leading.reshape(row_count * tile_len, feat)[:2 * tile_len]
    hi, lo = factor(front)
    gathered = lax.all_gather(unit, "col", axis=2, tiled=True)
    stride = col_count // row_count
    grouped = gathered.reshape(local_tiles // stride, stride, tile_len, feat)
    chosen = lax.dynamic_index_in_dim(grouped, own_col // row_count, 1, keepdims=False)
    kept = jnp.where(own_row == own_col % row_count, chosen, 0).astype(BF)
    col_points = lax.psum(kept, "row").reshape(-1, feat)
    row_points = gathered.reshape(-1, feat)
    ids = jnp.stack(
        [own_row, jnp.int32(row_count), own_col, jnp.int32(col_count)]
    ).astype(jnp.int32)
    big, panels = schur(ids, row_points, col_points, front, hi, lo, tile_len)
    across = col_points.shape[0] // tile_len
    return (
        big.reshape(local_tiles, 1, tile_len, across, 1, tile_len),
        panels.reshape(local_tiles, 1, tile_len, 2 * tile_len),
    )


def solution(mesh):
    return jax.shard_map(
        per_device,
        mesh=mesh,
        in_specs=(P(None, "row", "col", None),),
        out_specs=(P(None, "row", None, None, "col", None), P(None, "row", None, None)),
        check_vma=False,
    )
```

time: 419 us -> 151 us (0.36); the launches traced: 411 us -> 151 us
  other arithmetic: 151 us -> 5.44 us
  matrix products: 102 us -> 0 us
  local copies, waits for them, and re-layouts: 103 us -> 1.46 us
  Pallas kernels: 0 us -> 65.7 us
  blocking collectives: 28.3 us -> 44.7 us
  waiting for transfers between devices: 8.71 us -> 19.3 us
    another operation x19 -> x1, other arithmetic: 120 us -> 0.59 us  [per_device(): jnp.stack([own_row, jnp.int32(row_count), own_col, jnp.int32(col_count)])]
    dot_general x8 -> x0, matrix products: 73.3 us -> none  [the longest x1 33.5 us: per_device(): lax.dot_general(both_rows, both_cols, (((1,), (1,)), ((), ())), precision...]
    pallas_call x0 -> x2, Pallas kernels: none -> 65.7 us  [the longest x1 45.5 us: schur(): pl.pallas_call(schur_body, out_shape=(jax.ShapeDtypeStruct((rows * chunks...]
    unnamed x54 -> x0, local copies, waits for them, and re-layouts: 28.9 us -> none
    another operation x19 -> x0, matrix products: 28.6 us -> none  [the longest x6 12.3 us: both_factors(): lax.linalg.triangular_solve(second_factor, reduced, left_side=False, lowe...]
    reshape x1 -> x0, local copies, waits for them, and re-layouts: 27.8 us -> none  [per_device(): schur.reshape(local_tiles, 1, tile_len, across_tiles, 1, tile_len)]
    broadcast_in_dim x24 -> x0, local copies, waits for them, and re-layouts: 22.2 us -> none  [the longest x16 20.7 us: mark_tiles(): jnp.where(marker == panel_index, factor[None], jnp.where(marker < panel_i...]
    all_gather x1, blocking collectives: 28.3 us -> 44.7 us  [per_device(): leading = lax.all_gather(unit[0, 0], ('row', 'col'))]
  transfers between devices with their start and end apart: 2 -> 2, of which waited for: 1 -> 1; matrix products, arithmetic and copies ran while one was open for 20% -> 1% of each run, Pallas kernels for 0% -> 13%
where the time goes in v1:
time: 151 us
  Pallas kernels  65.7 us (44%)
  blocking collectives  44.7 us (30%)
  waiting for transfers between devices  19.3 us (13%)
  between operations  14.1 us (9%)
  other arithmetic  5.44 us (4%)
    pallas_call x1, Pallas kernels, schur(): pl.pallas_call(schur_body, out_shape=(jax.ShapeDtypeStruct((rows * chunks...  45.5 us
    all_gather x1, blocking collectives, per_device(): leading = lax.all_gather(unit[0, 0], ('row', 'col'))  44.7 us
    pallas_call x1, Pallas kernels, factor(): pl.pallas_call(factor_body, out_shape=(shape, shape), in_specs=[pl.BlockS...  20.3 us
    psum x1, waiting for transfers between devices, per_device(): col_points = lax.psum(kept, 'row').reshape(-1, feat)  19.3 us
  transfers between devices with their start and end apart: 2, of which 1 were waited for; matrix products, arithmetic and copies ran while one was open for 1% of the time, Pallas kernels for 13%

profile of v1, /device:TPU:0, one launch (start us, length us, event | category | flops | bytes accessed | tf_op | source)
XLA Modules:
  0.0 150.9 jit_solution(12101271653965134298)
XLA Ops:
  7.2 0.0 all-gather.3.cloned.1.call-start
  7.2 1.1 fusion
  8.3 1.7 %fusion.1 = bf16[12,1,32,256]{3,2,1,0:T(8,128)(2,1)} fusion(bf16[12,1,32,256]{3,2,1,0:T(8,128)(2,1)} %param.1, f32[12,32]{1,0:T(8,128)S(1)} %add_rsqrt_fusion), kind=kLoop, calls=%fused_computation.4 | loop fusion | flops 294912 | bytes 394752 | tf_op jit(solution)/shard_map/convert_element_type | solution.py:239
  10.0 0.0 all-gather.3.cloned.1.call-update
  10.0 0.0 all-reduce.2.cloned.1.call-start
  10.1 0.7 slice.13
  10.8 44.7 %all-gather = bf16[32,1,32,256]{3,2,1,0:T(8,128)(2,1)S(1)} all-gather(bf16[1,1,32,256]{3,2,1,0:T(8,128)(2,1)S(1)} %slice.13), channel_id=2, replica_groups=mesh['row'=4,'col'=8] {'row','col'}, dimensions={0}, use_global_device_ids=true | all-gather | bytes 540672 | tf_op jit(solution)/shard_map/all_gather | solution.py:240
  55.6 0.7 slice.14
  56.3 0.0 all-gather.3.cloned.1.call-done
  56.3 2.1 %bitcast_select_fusion = bf16[6,1,256,256]{3,2,0,1:T(8,128)(2,1)} fusion(bf16[6,2,256,256]{3,2,1,0:T(8,128)(2,1)} %bitcast.12, s32[]{:T(128)S(6)} %select_n.29, pred[]{:T(512)S(6)} %eq.5), kind=kLoop, calls=%fused_computation | loop fusion | flops 393216 | bytes 1572869 | tf_op jit(solution)/shard_map/jit(_where)/select_n | solution.py:250
  58.4 0.0 all-reduce.2.cloned.1.call-update
  58.4 20.3 %factor.1 = (bf16[512,512]{1,0:T(8,128)(2,1)}, bf16[512,512]{1,0:T(8,128)(2,1)}) custom-call(bf16[512,256]{1,0:T(8,128)(2,1)} %bitcast.15), custom_call_target="tpu_custom_call" | custom-call | flops 20000000000 | bytes 50000000 | tf_op jit(solution)/shard_map/factor/pallas_call | solution.py:129
  78.7 0.6 pad_add_fusion.ids
  79.2 19.3 %all-reduce.2.cloned.1.call-done.cols_ref = bf16[1536,256]{1,0:T(8,128)(2,1)} async-done(((bf16[1536,256]{1,0:T(8,128)(2,1)}), bf16[1536,256]{1,0:T(8,128)(2,1)}) %all-reduce.2.cloned.1.call-update) | async-done | bytes 786448 | tf_op jit(solution)/shard_map/psum | solution.py:251
  98.5 45.5 %schur.1 = (f32[36864,128]{1,0:T(8,128)}, f32[3072,512]{1,0:T(8,128)}) custom-call(s32[4]{0:T(128)} %pad_add_fusion.ids, bf16[3072,256]{1,0:T(8,128)(2,1)} %bitcast.13, bf16[1536,256]{1,0:T(8,128)(2,1)} %all-reduce.2.cloned.1.call-done.cols_ref, bf16[512,256]{1,0:T(8,128)(2,1)} %bitcast.16, bf16[512,512]{1,0:T(8,128)(2,1)} %get-tuple-element.6.hi_ref, ...), custom_call_target="tpu_custom_call" | custom-call | tf_op jit(solution)/shard_map/schur/pallas_call | solution.py:204
  (1 shorter events, 0.0 us)
Async XLA Ops:
  7.2 49.1 %all-gather.3.cloned.1.call-start = ((), (), s32[]{:S(2)}) async-start(), calls=%async_computation | async-start | bytes 1769472 | tf_op jit(solution)/shard_map/all_gather | solution.py:246
  10.0 88.5 %all-reduce.2.cloned.1.call-start = ((), (), s32[]{:S(2)}) async-start(), calls=%async_computation.1 | async-start | bytes 1572864 | tf_op jit(solution)/shard_map/psum | solution.py:251
Sparse Core Ops, SparseCore 0:
  10.4 29.6 all-gather.2
  58.5 39.9 all-reduce.1

commit v2 on v1

--- a/solution.py
+++ b/solution.py
@@ -1,4 +1,3 @@
-import functools
 import math
 
 import jax
@@ -137,6 +136,151 @@
     )(front)
 
 
+def exchange_body(
+    unit_ref, cols_ref, front_ref, held, own_sem, up_send, up_recv, dn_send, dn_recv, col_send,
+    col_recv, front_send, front_recv, keep_sem,
+):
+    rows = lax.axis_size("row")
+    peers = lax.axis_size("col")
+    r = lax.axis_index("row")
+    c = lax.axis_index("col")
+    piece = unit_ref.shape[2]
+
+    barrier = pltpu.get_barrier_semaphore()
+    for d in range(1, rows):
+        pl.semaphore_signal(
+            barrier, inc=1, device_id=(lax.rem(r + d, rows), c),
+            device_id_type=pl.DeviceIdType.MESH,
+        )
+    for d in range(1, peers):
+        pl.semaphore_signal(
+            barrier, inc=1, device_id=(r, lax.rem(c + d, peers)),
+            device_id_type=pl.DeviceIdType.MESH,
+        )
+    pl.semaphore_wait(barrier, rows + peers - 2)
+
+    own = pltpu.make_async_copy(unit_ref, held.at[r], own_sem)
+    own.start()
+    own.wait()
+
+    def hop(block, target, send, recv):
+        return pltpu.make_async_remote_copy(
+            src_ref=held.at[block], dst_ref=held.at[block], send_sem=send, recv_sem=recv,
+            device_id=(target, c), device_id_type=pl.DeviceIdType.MESH,
+        )
+
+    def up(step):
+        return hop(r - step, r + 1, up_send.at[step], up_recv.at[step])
+
+    def down(step):
+        return hop(r + step, r - 1, dn_send.at[step], dn_recv.at[step])
+
+    def arrived_up(step):
+        return hop(r - 1 - step, r - 1, up_send.at[step], up_recv.at[step])
+
+    def arrived_down(step):
+        return hop(r + 1 + step, r + 1, dn_send.at[step], dn_recv.at[step])
+
+    for step in range(rows - 1):
+        @pl.when((r + 1 < rows) & (r - step >= 0))
+        def _():
+            up(step).start()
+
+        @pl.when((r - 1 >= 0) & (r + step < rows))
+        def _():
+            down(step).start()
+
+        @pl.when(r - 1 - step >= 0)
+        def _():
+            arrived_up(step).wait_recv()
+
+        @pl.when(r + 1 + step < rows)
+        def _():
+            arrived_down(step).wait_recv()
+
+    here = pl.ds(pl.multiple_of(c * piece, piece), piece)
+    front_src = held.at[0:2, 0, 0]
+    front_dst = front_ref.at[:, here]
+    copies = []
+    for d in range(1, peers):
+        peer = lax.rem(c + d, peers)
+        copies.append(
+            pltpu.make_async_remote_copy(
+                src_ref=front_src, dst_ref=front_dst, send_sem=front_send.at[d],
+                recv_sem=front_recv.at[d], device_id=(r, peer),
+                device_id_type=pl.DeviceIdType.MESH,
+            )
+        )
+        copies.append(
+            pltpu.make_async_remote_copy(
+                src_ref=held.at[lax.rem(peer, rows), :, peer // rows],
+                dst_ref=cols_ref.at[:, here], send_sem=col_send.at[d],
+                recv_sem=col_recv.at[d], device_id=(r, peer),
+                device_id_type=pl.DeviceIdType.MESH,
+            )
+        )
+    for copy in copies:
+        copy.start()
+    kept = [
+        pltpu.make_async_copy(front_src, front_dst, keep_sem.at[0]),
+        pltpu.make_async_copy(
+            held.at[lax.rem(c, rows), :, c // rows], cols_ref.at[:, here], keep_sem.at[1]
+        ),
+    ]
+    for copy in kept:
+        copy.start()
+    for copy in kept:
+        copy.wait()
+    for copy in copies:
+        copy.wait_send()
+    for d in range(1, peers):
+        peer = lax.rem(c - d + peers, peers)
+        there = pl.ds(pl.multiple_of(peer * piece, piece), piece)
+        pltpu.make_async_remote_copy(
+            src_ref=front_src, dst_ref=front_ref.at[:, there], send_sem=front_send.at[d],
+            recv_sem=front_recv.at[d], device_id=(r, peer), device_id_type=pl.DeviceIdType.MESH,
+        ).wait_recv()
+        pltpu.make_async_remote_copy(
+            src_ref=held.at[lax.rem(c, rows), :, c // rows], dst_ref=cols_ref.at[:, there],
+            send_sem=col_send.at[d], recv_sem=col_recv.at[d], device_id=(r, peer),
+            device_id_type=pl.DeviceIdType.MESH,
+        ).wait_recv()
+    for step in range(rows - 1):
+        @pl.when((r + 1 < rows) & (r - step >= 0))
+        def _():
+            up(step).wait_send()
+
+        @pl.when((r - 1 >= 0) & (r + step < rows))
+        def _():
+            down(step).wait_send()
+
+
+def exchange(unit, row_count, col_count):
+    local_tiles, piece, feat = unit.shape
+    stride = col_count // row_count
+    across = local_tiles // stride
+    tile_len = piece * col_count
+    dma = pltpu.SemaphoreType.DMA
+    anywhere = pl.BlockSpec(memory_space=pl.ANY)
+    return pl.pallas_call(
+        exchange_body,
+        out_shape=(
+            jax.ShapeDtypeStruct((across, tile_len, feat), BF),
+            jax.ShapeDtypeStruct((2, tile_len, feat), BF),
+        ),
+        in_specs=[anywhere],
+        out_specs=(anywhere, anywhere),
+        scratch_shapes=[
+            pltpu.VMEM((row_count, across, stride, piece, feat), BF),
+            dma, dma((row_count,)), dma((row_count,)), dma((row_count,)), dma((row_count,)),
+            dma((col_count,)), dma((col_count,)), dma((col_count,)), dma((col_count,)), dma((2,)),
+        ],
+        compiler_params=pltpu.CompilerParams(collective_id=0, has_side_effects=True),
+        cost_estimate=pl.CostEstimate(flops=int(2e10), bytes_accessed=int(5e7), transcendentals=0),
+        name="exchange",
+    )(unit.reshape(across, stride, piece, feat))
+
+
 def panel_of(points, tile_id, front, hi_ref, lo_ref, tile_len):
     n = front.shape[0]
     values = gram(points, front)
@@ -237,18 +381,13 @@
     unit = (
         floated * lax.rsqrt(jnp.sum(floated * floated, axis=-1, keepdims=True) + epsilon)
     ).astype(BF)
-    leading = lax.all_gather(unit[0, 0], ("row", "col"))
-    piece, feat = leading.shape[1:]
-    local_tiles = unit.shape[0]
+    local_tiles, _, piece, feat = unit.shape
     tile_len = piece * col_count
-    front = leading.reshape(row_count * tile_len, feat)[:2 * tile_len]
+    gathered = lax.all_gather(unit, "col", axis=2, tiled=True)
+    cols, leading = exchange(unit[:, 0], row_count, col_count)
+    front = leading.reshape(2 * tile_len, feat)
+    col_points = cols.reshape(-1, feat)
     hi, lo = factor(front)
-    gathered = lax.all_gather(unit, "col", axis=2, tiled=True)
-    stride = col_count // row_count
-    grouped = gathered.reshape(local_tiles // stride, stride, tile_len, feat)
-    chosen = lax.dynamic_index_in_dim(grouped, own_col // row_count, 1, keepdims=False)
-    kept = jnp.where(own_row == own_col % row_count, chosen, 0).astype(BF)
-    col_points = lax.psum(kept, "row").reshape(-1, feat)
     row_points = gathered.reshape(-1, feat)
     ids = jnp.stack(
         [own_row, jnp.int32(row_count), own_col, jnp.int32(col_count)]

time: 151 us -> 122 us (0.81); the launches traced: 151 us -> 120 us
  blocking collectives: 44.7 us -> 0 us
  Pallas kernels: 65.7 us -> 103 us
  waiting for transfers between devices: 19.3 us -> 0.02 us
  other arithmetic: 5.44 us -> 3.43 us
    all_gather x1 -> x0, blocking collectives: 44.7 us -> none  [per_device(): leading = lax.all_gather(unit[0, 0], ('row', 'col'))]
    pallas_call x0 -> x1, Pallas kernels: none -> 37 us  [exchange(): pl.pallas_call(exchange_body, out_shape=(jax.ShapeDtypeStruct((across, ti...]
    psum x1 -> x0, waiting for transfers between devices: 19.3 us -> none  [per_device(): col_points = lax.psum(kept, 'row').reshape(-1, feat)]
    select_n x1 -> x0, other arithmetic: 2.07 us -> none  [per_device(): kept = jnp.where(own_row == own_col % row_count, chosen, 0).astype(BF)]
  transfers between devices with their start and end apart: 2 -> 1, of which waited for: 1 -> 0; matrix products, arithmetic and copies ran while one was open for 1% -> 1% of each run, Pallas kernels for 13% -> 48%
where the time goes in v2:
time: 122 us; the launch traced here: 120 us
  Pallas kernels  103 us (84%)
  between operations  14.1 us (12%)
  other arithmetic  3.43 us (3%)
    pallas_call x1, Pallas kernels, schur(): pl.pallas_call(schur_body, out_shape=(jax.ShapeDtypeStruct((rows * chunks...  45.5 us
    pallas_call x1, Pallas kernels, exchange(): pl.pallas_call(exchange_body, out_shape=(jax.ShapeDtypeStruct((across, ti...  37 us
    pallas_call x1, Pallas kernels, factor(): pl.pallas_call(factor_body, out_shape=(shape, shape), in_specs=[pl.BlockS...  20.3 us
  transfers between devices with their start and end apart: 1, of which 0 were waited for; matrix products, arithmetic and copies ran while one was open for 1% of the time, Pallas kernels for 48%

profile of v2, /device:TPU:0, one launch (start us, length us, event | category | flops | bytes accessed | tf_op | source)
XLA Modules:
  0.0 120.3 jit_solution(15535499490885553357)
XLA Ops:
  7.2 0.0 all-gather.2.cloned.1.call-start
  7.2 1.1 fusion
  8.3 1.7 %fusion.1 = bf16[12,1,32,256]{3,2,1,0:T(8,128)(2,1)} fusion(bf16[12,1,32,256]{3,2,1,0:T(8,128)(2,1)} %param.1, f32[12,32]{1,0:T(8,128)S(1)} %add_rsqrt_fusion), kind=kLoop, calls=%fused_computation.3 | loop fusion | flops 294912 | bytes 394752 | tf_op jit(solution)/shard_map/convert_element_type | solution.py:383
  10.0 0.0 all-gather.2.cloned.1.call-update
  10.0 37.0 %exchange.1 = (bf16[6,256,256]{2,1,0:T(8,128)(2,1)}, bf16[2,256,256]{2,1,0:T(8,128)(2,1)}) custom-call(bf16[6,2,32,256]{3,2,1,0:T(8,128)(2,1)} %bitcast.11), custom_call_target="tpu_custom_call" | custom-call | flops 20000000000 | bytes 50000000 | tf_op jit(solution)/shard_map/exchange/pallas_call | solution.py:265
  47.1 0.7 pad_add_fusion.ids
  47.7 20.3 %factor.1 = (bf16[512,512]{1,0:T(8,128)(2,1)}, bf16[512,512]{1,0:T(8,128)(2,1)}) custom-call(bf16[512,256]{1,0:T(8,128)(2,1)} %bitcast.13), custom_call_target="tpu_custom_call" | custom-call | flops 20000000000 | bytes 50000000 | tf_op jit(solution)/shard_map/factor/pallas_call | solution.py:128
  68.0 0.0 all-gather.2.cloned.1.call-done
  68.0 45.5 %schur.1 = (f32[36864,128]{1,0:T(8,128)}, f32[3072,512]{1,0:T(8,128)}) custom-call(s32[4]{0:T(128)} %pad_add_fusion.ids, bf16[3072,256]{1,0:T(8,128)(2,1)} %bitcast.10, bf16[1536,256]{1,0:T(8,128)(2,1)} %bitcast.12, bf16[512,256]{1,0:T(8,128)(2,1)} %bitcast.14, bf16[512,512]{1,0:T(8,128)(2,1)} %get-tuple-element.10.hi_ref, ...), custom_call_target="tpu_custom_call" | custom-call | tf_op jit(solution)/shard_map/schur/pallas_call | solution.py:348
  (1 shorter events, 0.0 us)
Async XLA Ops:
  7.2 60.8 %all-gather.2.cloned.1.call-start = ((), (), s32[]{:S(2)}) async-start(), calls=%async_computation | async-start | bytes 1769472 | tf_op jit(solution)/shard_map/all_gather | solution.py:386
Sparse Core Ops, SparseCore 0:
  10.4 37.5 all-gather.1

commit v3 on v2

--- a/solution.py
+++ b/solution.py
@@ -322,12 +322,11 @@
     hi, lo = split(panel)
     p = jnp.concatenate([hi, hi[:, :LEAF], lo[:, :LEAF]], axis=1)
     per = tile_len // LEAF
+    s = gram(points, cols_ref[...]) - dot(p, q_ref[...], NT)
+    for k in range(chunks):
+        out_ref[pl.ds(k, tile_len, stride=chunks), :] = s[:, k * LEAF:(k + 1) * LEAF]
+
     for b in range(across):
-        here = slice(b * tile_len, (b + 1) * tile_len)
-        s = gram(points, cols_ref[here, :]) - dot(p, q_ref[here, :], NT)
-        for k in range(per):
-            out_ref[pl.ds(b * per + k, tile_len, stride=chunks), :] = s[:, k * LEAF:(k + 1) * LEAF]
-
         @pl.when(tile_id == b * col_count + own_col)
         def _():
             ident = eye(tile_len)

time: 122 us -> 103 us (0.84)
  Pallas kernels: 103 us -> 83.7 us
    pallas_call x1, Pallas kernels: 45.5 us -> 26.4 us  [schur(): pl.pallas_call(schur_body, out_shape=(jax.ShapeDtypeStruct((rows * chunks...]
  transfers between devices with their start and end apart: 1 -> 1, of which waited for: 0 -> 0; matrix products, arithmetic and copies ran while one was open for 1% -> 1% of each run, Pallas kernels for 48% -> 57%
where the time goes in v3:
time: 103 us; the launch traced here: 101 us
  Pallas kernels  83.7 us (81%)
  between operations  14.1 us (14%)
  other arithmetic  3.43 us (3%)
    pallas_call x1, Pallas kernels, exchange(): pl.pallas_call(exchange_body, out_shape=(jax.ShapeDtypeStruct((across, ti...  37 us
    pallas_call x1, Pallas kernels, schur(): pl.pallas_call(schur_body, out_shape=(jax.ShapeDtypeStruct((rows * chunks...  26.4 us
    pallas_call x1, Pallas kernels, factor(): pl.pallas_call(factor_body, out_shape=(shape, shape), in_specs=[pl.BlockS...  20.3 us
  transfers between devices with their start and end apart: 1, of which 0 were waited for; matrix products, arithmetic and copies ran while one was open for 1% of the time, Pallas kernels for 57%

profile of v3, /device:TPU:0, one launch (start us, length us, event | category | flops | bytes accessed | tf_op | source)
XLA Modules:
  0.0 101.3 jit_solution(15758708396048323751)
XLA Ops:
  7.2 0.0 all-gather.2.cloned.1.call-start
  7.2 1.1 %fusion = f32[12,32]{1,0:T(8,128)S(1)} fusion(bf16[12,1,32,256]{3,2,1,0:T(8,128)(2,1)} %param.1), kind=kLoop, calls=%fused_computation.2 | loop fusion | flops 294528 | bytes 198144 | tf_op jit(solution)/shard_map/reduce_sum | solution.py:381
  8.3 1.7 %fusion.1 = bf16[12,1,32,256]{3,2,1,0:T(8,128)(2,1)} fusion(bf16[12,1,32,256]{3,2,1,0:T(8,128)(2,1)} %param.1, f32[12,32]{1,0:T(8,128)S(1)} %add_rsqrt_fusion), kind=kLoop, calls=%fused_computation.3 | loop fusion | flops 294912 | bytes 394752 | tf_op jit(solution)/shard_map/convert_element_type | solution.py:382
  10.0 0.0 all-gather.2.cloned.1.call-update
  10.0 37.0 %exchange.1 = (bf16[6,256,256]{2,1,0:T(8,128)(2,1)}, bf16[2,256,256]{2,1,0:T(8,128)(2,1)}) custom-call(bf16[6,2,32,256]{3,2,1,0:T(8,128)(2,1)} %bitcast.11), custom_call_target="tpu_custom_call" | custom-call | flops 20000000000 | bytes 50000000 | tf_op jit(solution)/shard_map/exchange/pallas_call | solution.py:265
  47.1 0.7 pad_add_fusion.ids
  47.7 20.3 %factor.1 = (bf16[512,512]{1,0:T(8,128)(2,1)}, bf16[512,512]{1,0:T(8,128)(2,1)}) custom-call(bf16[512,256]{1,0:T(8,128)(2,1)} %bitcast.13), custom_call_target="tpu_custom_call" | custom-call | flops 20000000000 | bytes 50000000 | tf_op jit(solution)/shard_map/factor/pallas_call | solution.py:128
  68.0 0.0 all-gather.2.cloned.1.call-done
  68.0 26.4 %schur.1 = (f32[36864,128]{1,0:T(8,128)}, f32[3072,512]{1,0:T(8,128)}) custom-call(s32[4]{0:T(128)} %pad_add_fusion.ids, bf16[3072,256]{1,0:T(8,128)(2,1)} %bitcast.10, bf16[1536,256]{1,0:T(8,128)(2,1)} %bitcast.12, bf16[512,256]{1,0:T(8,128)(2,1)} %bitcast.14, bf16[512,512]{1,0:T(8,128)(2,1)} %get-tuple-element.10.hi_ref, ...), custom_call_target="tpu_custom_call" | custom-call | tf_op jit(solution)/shard_map/schur/pallas_call | solution.py:347
  (1 shorter events, 0.0 us)
Async XLA Ops:
  7.2 60.8 %all-gather.2.cloned.1.call-start = ((), (), s32[]{:S(2)}) async-start(), calls=%async_computation | async-start | bytes 1769472 | tf_op jit(solution)/shard_map/all_gather | solution.py:385
Sparse Core Ops, SparseCore 0:
  10.4 37.5 all-gather.1

commit v4 on v3

--- a/solution.py
+++ b/solution.py
@@ -181,6 +181,21 @@
     def arrived_down(step):
         return hop(r + 1 + step, r + 1, dn_send.at[step], dn_recv.at[step])
 
+    here = pl.ds(pl.multiple_of(c * piece, piece), piece)
+
+    def hand_out(block):
+        for turn in range(unit_ref.shape[1]):
+            peer = block + turn * rows
+            away = lax.rem(peer - c + peers, peers)
+
+            @pl.when(peer != c)
+            def _():
+                pltpu.make_async_remote_copy(
+                    src_ref=held.at[block, :, turn], dst_ref=cols_ref.at[:, here],
+                    send_sem=col_send.at[away], recv_sem=col_recv.at[away],
+                    device_id=(r, peer), device_id_type=pl.DeviceIdType.MESH,
+                ).start()
+
     for step in range(rows - 1):
         @pl.when((r + 1 < rows) & (r - step >= 0))
         def _():
@@ -190,15 +205,19 @@
         def _():
             down(step).start()
 
+        if step == 0:
+            hand_out(r)
+
         @pl.when(r - 1 - step >= 0)
         def _():
             arrived_up(step).wait_recv()
+            hand_out(r - 1 - step)
 
         @pl.when(r + 1 + step < rows)
         def _():
             arrived_down(step).wait_recv()
-
-    here = pl.ds(pl.multiple_of(c * piece, piece), piece)
+            hand_out(r + 1 + step)
+
     front_src = held.at[0:2, 0, 0]
     front_dst = front_ref.at[:, here]
     copies = []
@@ -219,7 +238,7 @@
                 device_id_type=pl.DeviceIdType.MESH,
             )
         )
-    for copy in copies:
+    for copy in copies[::2]:
         copy.start()
     kept = [
         pltpu.make_async_copy(front_src, front_dst, keep_sem.at[0]),
@@ -313,7 +332,7 @@
             q_ref[here, :] = jnp.concatenate([hi, lo[:, :LEAF], hi[:, :LEAF]], axis=1)
             return carry
 
-        lax.fori_loop(0, across, one, 0)
+        lax.fori_loop(0, across, one, 0, unroll=True)
 
     tile_id = a * row_count + own_row
     points = rows_ref[...]

time: 103 us -> 97.2 us (0.944); the launches traced: 101 us -> 96.9 us
  Pallas kernels: 83.7 us -> 79.4 us
    pallas_call x1, Pallas kernels: 37 us -> 34.2 us  [exchange(): pl.pallas_call(exchange_body, out_shape=(jax.ShapeDtypeStruct((across, ti...]
    pallas_call x1, Pallas kernels: 26.4 us -> 24.9 us  [schur(): pl.pallas_call(schur_body, out_shape=(jax.ShapeDtypeStruct((rows * chunks...]
  transfers between devices with their start and end apart: 1 -> 1, of which waited for: 0 -> 0; matrix products, arithmetic and copies ran while one was open for 1% -> 1% of each run, Pallas kernels for 57% -> 56%
where the time goes in v4:
time: 97.2 us; the launch traced here: 96.9 us
  Pallas kernels  79.4 us (82%)
  between operations  14.1 us (15%)
  other arithmetic  3.43 us (4%)
    pallas_call x1, Pallas kernels, exchange(): pl.pallas_call(exchange_body, out_shape=(jax.ShapeDtypeStruct((across, ti...  34.2 us
    pallas_call x1, Pallas kernels, schur(): pl.pallas_call(schur_body, out_shape=(jax.ShapeDtypeStruct((rows * chunks...  24.9 us
    pallas_call x1, Pallas kernels, factor(): pl.pallas_call(factor_body, out_shape=(shape, shape), in_specs=[pl.BlockS...  20.3 us
  transfers between devices with their start and end apart: 1, of which 0 were waited for; matrix products, arithmetic and copies ran while one was open for 1% of the time, Pallas kernels for 56%

profile of v4, /device:TPU:0, one launch (start us, length us, event | category | flops | bytes accessed | tf_op | source)
XLA Modules:
  0.0 96.9 jit_solution(6543490105359666803)
XLA Ops:
  7.2 0.0 all-gather.2.cloned.1.call-start
  7.2 1.1 %fusion = f32[12,32]{1,0:T(8,128)S(1)} fusion(bf16[12,1,32,256]{3,2,1,0:T(8,128)(2,1)} %param.1), kind=kLoop, calls=%fused_computation.2 | loop fusion | flops 294528 | bytes 198144 | tf_op jit(solution)/shard_map/reduce_sum | solution.py:400
  8.3 1.7 %fusion.1 = bf16[12,1,32,256]{3,2,1,0:T(8,128)(2,1)} fusion(bf16[12,1,32,256]{3,2,1,0:T(8,128)(2,1)} %param.1, f32[12,32]{1,0:T(8,128)S(1)} %add_rsqrt_fusion), kind=kLoop, calls=%fused_computation.3 | loop fusion | flops 294912 | bytes 394752 | tf_op jit(solution)/shard_map/convert_element_type | solution.py:401
  10.0 0.0 all-gather.2.cloned.1.call-update
  10.0 34.2 %exchange.1 = (bf16[6,256,256]{2,1,0:T(8,128)(2,1)}, bf16[2,256,256]{2,1,0:T(8,128)(2,1)}) custom-call(bf16[6,2,32,256]{3,2,1,0:T(8,128)(2,1)} %bitcast.11), custom_call_target="tpu_custom_call" | custom-call | flops 20000000000 | bytes 50000000 | tf_op jit(solution)/shard_map/exchange/pallas_call | solution.py:284
  44.2 0.7 pad_add_fusion.ids
  44.9 20.3 %factor.1 = (bf16[512,512]{1,0:T(8,128)(2,1)}, bf16[512,512]{1,0:T(8,128)(2,1)}) custom-call(bf16[512,256]{1,0:T(8,128)(2,1)} %bitcast.13), custom_call_target="tpu_custom_call" | custom-call | flops 20000000000 | bytes 50000000 | tf_op jit(solution)/shard_map/factor/pallas_call | solution.py:128
  65.1 0.0 all-gather.2.cloned.1.call-done
  65.1 24.9 %schur.1 = (f32[36864,128]{1,0:T(8,128)}, f32[3072,512]{1,0:T(8,128)}) custom-call(s32[4]{0:T(128)} %pad_add_fusion.ids, bf16[3072,256]{1,0:T(8,128)(2,1)} %bitcast.10, bf16[1536,256]{1,0:T(8,128)(2,1)} %bitcast.12, bf16[512,256]{1,0:T(8,128)(2,1)} %bitcast.14, bf16[512,512]{1,0:T(8,128)(2,1)} %get-tuple-element.10.hi_ref, ...), custom_call_target="tpu_custom_call" | custom-call | tf_op jit(solution)/shard_map/schur/pallas_call | solution.py:366
  (1 shorter events, 0.0 us)
Async XLA Ops:
  7.2 57.9 %all-gather.2.cloned.1.call-start = ((), (), s32[]{:S(2)}) async-start(), calls=%async_computation | async-start | bytes 1769472 | tf_op jit(solution)/shard_map/all_gather | solution.py:404
Sparse Core Ops, SparseCore 0:
  10.4 32.0 all-gather.1
